TPU v7x, 256 devices: a whole 4x4x8 slice. The times are simulated.
256 devices in a mesh: row: 32 (over z, y), col: 8 (over x, core).
Axes of the slice: x: 4, y: 4, z: 8, core: 2. Of those that a mesh axis runs over, the one named last changes fastest.
Arguments:
- expression: bfloat16 [32768, 1024], P(('row', 'col')), as said below
- power_order: int32 [20], replicated, may hold values from 0 to 19, each once
Outputs:
- log_conn: float32 [32768, 20], P(('row', 'col'))
- fit: float32 [20], replicated
- slope: float32 [20], replicated
Inputs may be any that keep to these rules, and one draw needn't show every extreme that they name: `expression`: each gene's row has mean zero and unit variance over the samples, up to rounding.
All inputs are finite; a program needn't handle non-finite values.
Results may differ from a plain program's by a relative error of at most 0.0029.
Values may be sent and summed in bfloat16 or wider, within the bound.
A program may use at most 64 MiB of HBM per device.

v0:
```python
import functools
import math
import jax
import jax.numpy as jnp
from jax import lax
from jax.sharding import Mesh
from jax.sharding import PartitionSpec as P

ROW = ("row_0", "row_1")
COL = ("col_0", "col_1")
ROW_COL = ("row_0", "row_1", "col_0", "col_1")


def from_everyone(x, axis):
    copies = jnp.broadcast_to(x, (lax.axis_size(axis), *x.shape))
    return lax.all_to_all(copies, axis, split_axis=0, concat_axis=0, tiled=True)


def in_order(tiles, dim):
    tiles = jnp.moveaxis(tiles, 0, dim)
    lengths = tiles.shape
    return tiles.reshape(*lengths[:dim], lengths[dim] * lengths[dim + 1], *lengths[dim + 2 :])


def gather_directly(x, axis, dim):
    tiles = from_everyone(x, axis)
    return in_order(tiles, dim)


def cut_along(x, dim, devices):
    lengths = x.shape
    tiles = x.reshape(*lengths[:dim], devices, lengths[dim] // devices, *lengths[dim + 1 :])
    return jnp.moveaxis(tiles, dim, 0)


def sum_at_owner(x, axis, dim):
    tiles = cut_along(x, dim, lax.axis_size(axis))
    arrived = lax.all_to_all(tiles, axis, split_axis=0, concat_axis=0, tiled=True)
    return arrived.sum(axis=0)


def over_axes(x, axes):
    return functools.reduce(lax.psum, axes, x)


def power_sums(rows, partners, samples, powers):
    corr = (
        lax.dot_general(
            rows, partners, (((1,), (1,)), ((), ())), preferred_element_type=jnp.float32
        )
        / samples
    )
    magnitude = jnp.abs(corr)
    current = magnitude
    sums = []
    for power in range(powers):
        sums.append(jnp.sum(current, axis=1))
        current = current * magnitude
    return jnp.stack(sums, axis=1)


def scale_free_fit(hist, log_total, bins):
    centers = jnp.arange(bins, dtype=jnp.float32) * (log_total / (bins - 1))
    weight_sum = jnp.sum(hist, axis=1, keepdims=True)
    ylog = jnp.log(hist + 1.0) - log_total
    xmean = jnp.sum(hist * centers[None, :], axis=1, keepdims=True) / weight_sum
    ymean = jnp.sum(hist * ylog, axis=1, keepdims=True) / weight_sum
    xdev = centers[None, :] - xmean
    ydev = ylog - ymean
    sxx = jnp.maximum(jnp.sum(hist * xdev * xdev, axis=1) / weight_sum[:, 0], 0.05)
    syy = jnp.maximum(jnp.sum(hist * ydev * ydev, axis=1) / weight_sum[:, 0], 0.05)
    sxy = jnp.sum(hist * xdev * ydev, axis=1) / weight_sum[:, 0]
    return (-sxy * jnp.abs(sxy) / (sxx * syy), sxy / sxx)


def on_device(expression, power_order):
    samples = expression.shape[1]
    powers = power_order.shape[0]
    bins = 128
    genes_total = expression.shape[0] * lax.axis_size(ROW) * lax.axis_size(COL)
    panel = gather_directly(expression, COL, 0)
    partial_value = power_sums(
        panel, lax.all_gather(expression, ROW, axis=0, tiled=True), samples, powers
    )
    conn = sum_at_owner(partial_value, COL, 0)
    selector = (power_order[:, None] == jnp.arange(powers, dtype=jnp.int32)[None, :]).astype(
        jnp.float32
    )
    picked = jnp.dot(conn, selector.T, precision=lax.Precision.HIGHEST)
    log_conn = jnp.log(picked)
    log_total = math.log(genes_total)
    position = log_conn * ((bins - 1) / log_total)
    levels = jnp.arange(bins, dtype=jnp.float32)
    weights = jnp.maximum(0.0, 1.0 - jnp.abs(position[:, :, None] - levels[None, None, :]))
    local_hist = jnp.sum(weights, axis=0)
    hist = over_axes(local_hist, ROW_COL)
    fit, slope = scale_free_fit(hist, log_total, bins)
    return (log_conn, fit, slope)


def solution(mesh):
    torus = Mesh(mesh.devices.reshape(8, 4, 4, 2), ("row_0", "row_1", "col_0", "col_1"))
    return jax.shard_map(
        on_device,
        mesh=torus,
        in_specs=(P(ROW_COL, None), P()),
        out_specs=(P(ROW_COL, None), P(), P()),
        check_vma=False,
    )
```

profile of v0, /device:TPU:1, one launch (start us, length us, event | category | flops | bytes accessed | tf_op | source)
XLA Modules:
  0.0 238.8 jit_solution(6960383103107341380)
XLA Ops:
  7.2 0.0 all-gather.2.cloned.1.call-start
  7.2 0.7 all-gather.2.cloned.1.call-update
  7.9 1.2 broadcast_in_dim.2
  9.1 31.9 %all_to_all.10 = bf16[8,128,1024]{2,1,0:T(8,128)(2,1)S(1)} all-to-all(bf16[8,128,1024]{2,1,0:T(8,128)(2,1)S(1)} %broadcast_in_dim.2), channel_id=1, replica_groups=mesh['row_0'=8,'row_1'=4,'col_0'=4,'col_1'=2] {'col_0','col_1'}, dimensions={0} | all-to-all | bytes 4194304 | tf_op jit(solution)/shard_map/all_to_all | solution.py:16
  41.0 70.6 %all-gather.2.cloned.1.call-done = bf16[4096,1024]{1,0:T(8,128)(2,1)} async-done(((bf16[128,1024]{1,0:T(8,128)(2,1)}), bf16[4096,1024]{1,0:T(8,128)(2,1)}) %all-gather.2.cloned.1.call-update) | async-done | bytes 8388624 | tf_op jit(solution)/shard_map/all_gather | solution.py:83
  111.5 0.0 copy-start
  111.5 43.9 %multiply_reduce_fusion = (f32[1024]{0:T(1024)S(1)}, f32[1024]{0:T(1024)S(1)}, f32[1024]{0:T(1024)S(1)}, f32[1024]{0:T(1024)S(1)}, f32[1024]{0:T(1024)S(1)}, /*i...) fusion(bf16[1024,1024]{1,0:T(8,128)(2,1)S(1)} %bitcast.44, ...), kind=kOutput, calls=%fused_computation | convolution fusion | flops 8761880576 | bytes 10567680 | tf_op jit(solution)/shard_map/dot_general | solution.py:48
  155.6 0.6 copy.10
  156.3 5.7 %all-to-all-start.1 = ((f32[8,128,20]{1,2,0:T(8,128)}), f32[8,128,20]{1,2,0:T(8,128)S(1)}, u32[]{:S(2)}, u32[]{:S(2)}) async-start(f32[8,128,20]{1,2,0:T(8,128)} %copy.10), calls=%async_computation.1 | async-start | bytes 196608 | tf_op jit(solution)/shard_map/all_to_all | solution.py:38
  161.9 5.0 %all-to-all-done.1 = f32[8,128,20]{1,2,0:T(8,128)S(1)} async-done(((f32[8,128,20]{1,2,0:T(8,128)}), f32[8,128,20]{1,2,0:T(8,128)S(1)}, u32[]{:S(2)}, u32[]{:S(2)}) %all-to-all-start.1) | async-done | bytes 81952 | tf_op jit(solution)/shard_map/all_to_all | solution.py:38
  166.9 0.0 copy-done
  166.9 0.8 broadcast_multiply_fusion
  167.7 0.4 maximum_reduce_fusion
  168.2 21.0 %psum.28 = f32[20,128]{1,0:T(8,128)S(1)} all-reduce(f32[20,128]{1,0:T(8,128)S(1)} %maximum_reduce_fusion), channel_id=1, replica_groups=mesh['row_0'=8,'row_1'=4,'col_0'=4,'col_1'=2] {'row_0'}, use_global_device_ids=true, to_apply=%region_22.0 | all-reduce | flops 2560 | bytes 20480 | tf_op jit(solution)/shard_map/psum | solution.py:43
  189.2 11.2 %psum.29 = f32[20,128]{1,0:T(8,128)S(1)} all-reduce(f32[20,128]{1,0:T(8,128)S(1)} %psum.28), channel_id=1, replica_groups=mesh['row_0'=8,'row_1'=4,'col_0'=4,'col_1'=2] {'row_1'}, use_global_device_ids=true, to_apply=%region_23.0 | all-reduce | flops 2560 | bytes 20480 | tf_op jit(solution)/shard_map/psum | solution.py:43
  200.3 11.6 %psum.30 = f32[20,128]{1,0:T(8,128)S(1)} all-reduce(f32[20,128]{1,0:T(8,128)S(1)} %psum.29), channel_id=1, replica_groups=mesh['row_0'=8,'row_1'=4,'col_0'=4,'col_1'=2] {'col_0'}, use_global_device_ids=true, to_apply=%region_24.0 | all-reduce | flops 2560 | bytes 20480 | tf_op jit(solution)/shard_map/psum | solution.py:43
  211.9 18.6 %psum.31 = f32[20,128]{1,0:T(8,128)S(1)} all-reduce(f32[20,128]{1,0:T(8,128)S(1)} %psum.30), channel_id=1, replica_groups=mesh['row_0'=8,'row_1'=4,'col_0'=4,'col_1'=2] {'col_1'}, use_global_device_ids=true, to_apply=%region_25.0 | all-reduce | flops 2560 | bytes 20480 | tf_op jit(solution)/shard_map/psum | solution.py:43
  230.5 0.2 multiply_reduce_fusion.11
  230.7 0.2 multiply_reduce_fusion.10
  230.9 0.5 multiply_divide_fusion
  231.4 0.5 multiply_divide_fusion.1
  (23 shorter events, 0.1 us)
Async XLA Ops:
  7.2 104.4 %all-gather.2.cloned.1.call-start = ((), (), s32[]{:S(2)}) async-start(), calls=%async_computation.2 | async-start | bytes 8650752 | tf_op jit(solution)/shard_map/all_gather | solution.py:83
  111.5 55.4 %copy-start = (s32[20]{0:T(128)S(1)}, s32[20]{0:T(128)}, u32[]{:S(2)}) copy-start(s32[20]{0:T(128)} %param.3) | copy-start | bytes 244
  156.3 10.6 %all-to-all-start.1 = ((f32[8,128,20]{1,2,0:T(8,128)}), f32[8,128,20]{1,2,0:T(8,128)S(1)}, u32[]{:S(2)}, u32[]{:S(2)}) async-start(f32[8,128,20]{1,2,0:T(8,128)} %copy.10), calls=%async_computation.1 | async-start | bytes 196608 | tf_op jit(solution)/shard_map/all_to_all | solution.py:38
Sparse Core Ops, SparseCore 0:
  10.6 100.9 all-gather.1
where the time goes:
time: 239 us
  blocking collectives  94.2 us (39%)
  waiting for transfers between devices  76.2 us (32%)
  matrix products  44.7 us (19%)
  between operations  14.2 us (6%)
  starting transfers between devices  5.69 us (2%)
    all_gather x1, waiting for transfers between devices, on_device(): lax.all_gather(expression, ROW, axis=0, tiled=True)  70.6 us
    psum x4, blocking collectives, over_axes(): return functools.reduce(lax.psum, axes, x)  62.3 us
    dot_general x1, matrix products, power_sums(): lax.dot_general(rows, partners, (((1,), (1,)), ((), ())), preferred_eleme...  43.9 us
    all_to_all x1, blocking collectives, from_everyone(): return lax.all_to_all(copies, axis, split_axis=0, concat_axis=0, tiled=True)  31.9 us
    all_to_all x1, starting transfers between devices, sum_at_owner(): lax.all_to_all(tiles, axis, split_axis=0, concat_axis=0, tiled=True)  5.66 us
    all_to_all x1, waiting for transfers between devices, sum_at_owner(): lax.all_to_all(tiles, axis, split_axis=0, concat_axis=0, tiled=True)  4.97 us
  transfers between devices with their start and end apart: 2, of which 2 were waited for; matrix products, arithmetic and copies ran while one was open for 1% of the time, Pallas kernels for 0%

commit v1 on v0

--- a/solution.py
+++ b/solution.py
@@ -80,7 +80,12 @@
     genes_total = expression.shape[0] * lax.axis_size(ROW) * lax.axis_size(COL)
     panel = gather_directly(expression, COL, 0)
     partial_value = power_sums(
-        panel, lax.all_gather(expression, ROW, axis=0, tiled=True), samples, powers
+        panel,
+        jnp.concatenate(
+            lax.all_to_all(jnp.stack([expression] * lax.axis_size(ROW)), ROW, 0, 0), axis=0
+        ),
+        samples,
+        powers,
     )
     conn = sum_at_owner(partial_value, COL, 0)
     selector = (power_order[:, None] == jnp.arange(powers, dtype=jnp.int32)[None, :]).astype(

time: 239 us -> 372 us (1.56)
  blocking collectives: 94.2 us -> 290 us
  waiting for transfers between devices: 76.2 us -> 4.99 us
  matrix products: 44.7 us -> 63.8 us
  between operations: 14.2 us -> 0.84 us
    all_to_all x0 -> x1, blocking collectives: none -> 194 us  [on_device(): lax.all_to_all(jnp.stack([expression] * lax.axis_size(ROW)), ROW, 0, 0)]
    all_gather x1 -> x0, waiting for transfers between devices: 70.6 us -> none  [on_device(): lax.all_gather(expression, ROW, axis=0, tiled=True)]
    dot_general x1, matrix products: 43.9 us -> 63 us  [power_sums(): lax.dot_general(rows, partners, (((1,), (1,)), ((), ())), preferred_eleme...]
  transfers between devices with their start and end apart: 2 -> 1, of which waited for: 2 -> 1; matrix products, arithmetic and copies ran while one was open for 1% -> 0% of each run, Pallas kernels for 0% -> 0%
where the time goes in v1:
time: 372 us
  blocking collectives  290 us (78%)
  matrix products  63.8 us (17%)
  starting transfers between devices  6.28 us (2%)
  waiting for transfers between devices  4.99 us (1%)
  local copies, waits for them, and re-layouts  3.92 us (1%)
    all_to_all x1, blocking collectives, on_device(): lax.all_to_all(jnp.stack([expression] * lax.axis_size(ROW)), ROW, 0, 0)  194 us
    psum x4, blocking collectives, over_axes(): return functools.reduce(lax.psum, axes, x)  63.8 us
    dot_general x1, matrix products, power_sums(): lax.dot_general(rows, partners, (((1,), (1,)), ((), ())), preferred_eleme...  63 us
    all_to_all x1, blocking collectives, from_everyone(): return lax.all_to_all(copies, axis, split_axis=0, concat_axis=0, tiled=True)  31.8 us
  transfers between devices with their start and end apart: 1, of which 1 were waited for; matrix products, arithmetic and copies ran while one was open for 0% of the time, Pallas kernels for 0%

profile of v1, /device:TPU:1, one launch (start us, length us, event | category | flops | bytes accessed | tf_op | source)
XLA Modules:
  0.0 371.5 jit_solution(13709309349299670378)
XLA Ops:
  0.6 1.2 broadcast_in_dim.2
  1.8 31.8 %all_to_all.15 = bf16[8,128,1024]{2,1,0:T(8,128)(2,1)S(1)} all-to-all(bf16[8,128,1024]{2,1,0:T(8,128)(2,1)S(1)} %broadcast_in_dim.2), channel_id=1, replica_groups=mesh['row_0'=8,'row_1'=4,'col_0'=4,'col_1'=2] {'col_0','col_1'}, dimensions={0} | all-to-all | bytes 4194304 | tf_op jit(solution)/shard_map/all_to_all | solution.py:16
  33.7 2.0 stack.44
  35.7 194.2 %all_to_all.16 = bf16[32,128,1024]{2,1,0:T(8,128)(2,1)S(1)} all-to-all(bf16[32,128,1024]{2,1,0:T(8,128)(2,1)S(1)} %stack.44), channel_id=1, replica_groups=mesh['row_0'=8,'row_1'=4,'col_0'=4,'col_1'=2] {'row_0','row_1'}, dimensions={0} | all-to-all | bytes 16777216 | tf_op jit(solution)/shard_map/all_to_all | solution.py:85
  229.9 0.0 copy-start
  229.9 63.0 %multiply_reduce_fusion = (f32[1024]{0:T(1024)S(1)}, f32[1024]{0:T(1024)S(1)}, f32[1024]{0:T(1024)S(1)}, f32[1024]{0:T(1024)S(1)}, f32[1024]{0:T(1024)S(1)}, /*i...) fusion(bf16[1024,1024]{1,0:T(8,128)(2,1)S(1)} %bitcast.46, ...), kind=kOutput, calls=%fused_computation | convolution fusion | flops 8761880576 | bytes 10567680 | tf_op jit(solution)/shard_map/dot_general | solution.py:48
  293.1 0.6 copy.10
  293.8 6.3 %all-to-all-start.2 = ((f32[8,128,20]{1,2,0:T(8,128)}), f32[8,128,20]{1,2,0:T(8,128)S(1)}, u32[]{:S(2)}, u32[]{:S(2)}) async-start(f32[8,128,20]{1,2,0:T(8,128)} %copy.10), calls=%async_computation.2 | async-start | bytes 196608 | tf_op jit(solution)/shard_map/all_to_all | solution.py:38
  300.1 5.0 %all-to-all-done.2 = f32[8,128,20]{1,2,0:T(8,128)S(1)} async-done(((f32[8,128,20]{1,2,0:T(8,128)}), f32[8,128,20]{1,2,0:T(8,128)S(1)}, u32[]{:S(2)}, u32[]{:S(2)}) %all-to-all-start.2) | async-done | bytes 81952 | tf_op jit(solution)/shard_map/all_to_all | solution.py:38
  305.1 0.0 copy-done
  305.1 0.8 broadcast_multiply_fusion
  305.9 0.4 maximum_reduce_fusion
  306.3 20.6 %psum.28 = f32[20,128]{1,0:T(8,128)S(1)} all-reduce(f32[20,128]{1,0:T(8,128)S(1)} %maximum_reduce_fusion), channel_id=1, replica_groups=mesh['row_0'=8,'row_1'=4,'col_0'=4,'col_1'=2] {'row_0'}, use_global_device_ids=true, to_apply=%region_22.0 | all-reduce | flops 2560 | bytes 20480 | tf_op jit(solution)/shard_map/psum | solution.py:43
  326.9 13.4 %psum.29 = f32[20,128]{1,0:T(8,128)S(1)} all-reduce(f32[20,128]{1,0:T(8,128)S(1)} %psum.28), channel_id=1, replica_groups=mesh['row_0'=8,'row_1'=4,'col_0'=4,'col_1'=2] {'row_1'}, use_global_device_ids=true, to_apply=%region_23.0 | all-reduce | flops 2560 | bytes 20480 | tf_op jit(solution)/shard_map/psum | solution.py:43
  340.3 11.5 %psum.30 = f32[20,128]{1,0:T(8,128)S(1)} all-reduce(f32[20,128]{1,0:T(8,128)S(1)} %psum.29), channel_id=1, replica_groups=mesh['row_0'=8,'row_1'=4,'col_0'=4,'col_1'=2] {'col_0'}, use_global_device_ids=true, to_apply=%region_24.0 | all-reduce | flops 2560 | bytes 20480 | tf_op jit(solution)/shard_map/psum | solution.py:43
  351.8 18.3 %psum.31 = f32[20,128]{1,0:T(8,128)S(1)} all-reduce(f32[20,128]{1,0:T(8,128)S(1)} %psum.30), channel_id=1, replica_groups=mesh['row_0'=8,'row_1'=4,'col_0'=4,'col_1'=2] {'col_1'}, use_global_device_ids=true, to_apply=%region_25.0 | all-reduce | flops 2560 | bytes 20480 | tf_op jit(solution)/shard_map/psum | solution.py:43
  370.1 0.2 multiply_reduce_fusion.11
  370.3 0.2 multiply_reduce_fusion.10
  370.5 0.5 multiply_divide_fusion
  371.0 0.5 multiply_divide_fusion.1
  (23 shorter events, 0.1 us)
Async XLA Ops:
  229.9 75.2 %copy-start = (s32[20]{0:T(128)S(1)}, s32[20]{0:T(128)}, u32[]{:S(2)}) copy-start(s32[20]{0:T(128)} %param.3) | copy-start | bytes 244
  293.8 11.3 %all-to-all-start.2 = ((f32[8,128,20]{1,2,0:T(8,128)}), f32[8,128,20]{1,2,0:T(8,128)S(1)}, u32[]{:S(2)}, u32[]{:S(2)}) async-start(f32[8,128,20]{1,2,0:T(8,128)} %copy.10), calls=%async_computation.2 | async-start | bytes 196608 | tf_op jit(solution)/shard_map/all_to_all | solution.py:38
